TPU v7x, 32 devices: a whole 2x2x4 slice. The times are simulated.
32 devices in a mesh: rep: 4 (over y, x), grp: 8 (over z, core).
Axes of the slice: x: 2, y: 2, z: 4, core: 2. Of those that a mesh axis runs over, the one named last changes fastest.
Arguments:
- block_in: bfloat16 [2, 4, 1024, 1024], P(None, 'rep', 'grp'), may hold values from -6 to 6
- cotangent: bfloat16 [2, 4, 1024, 1024], P(None, 'rep', 'grp'), may hold values from -6 to 6
- w_qkv: bfloat16 [2, 1024, 3072], P(None, 'grp'), may hold values from -0.1875 to 0.1875
- w_out: bfloat16 [2, 1024, 1024], P(None, 'grp'), may hold values from -0.1875 to 0.1875
- w_up: bfloat16 [2, 1024, 4096], P(None, 'grp'), may hold values from -0.1875 to 0.1875
- w_down: bfloat16 [2, 4096, 1024], P(None, 'grp'), may hold values from -0.09375 to 0.09375
- norm_gains: bfloat16 [2, 1024, 4], P(None, 'grp'), may hold values from 0.25 to 1.75
Outputs:
- block_out: bfloat16 [2, 4, 1024, 1024], P(None, 'rep', 'grp')
- block_in_grad: float32 [2, 4, 1024, 1024], P(None, 'rep', 'grp')
- w_qkv_grad: float32 [2, 1024, 3072], P(None, 'grp')
- w_out_grad: float32 [2, 1024, 1024], P(None, 'grp')
- w_up_grad: float32 [2, 1024, 4096], P(None, 'grp')
- w_down_grad: float32 [2, 4096, 1024], P(None, 'grp')
- norm_gains_grad: float32 [2, 1024, 4], P(None, 'grp')
All inputs are finite; a program needn't handle non-finite values.
Results may differ from a plain program's by a relative error of at most 0.023.
Values may be sent and summed in bfloat16 or wider, within the bound.
A program may use at most 384 MiB of HBM per device.

v0:
```python
import jax
import jax.numpy as jnp
from jax import lax
from jax.sharding import PartitionSpec as P

HEADS = 16
HDIM = 64
EPS = 1e-06
NEGATIVE = -1e30


def norm_apply(values, gains):
    return values * lax.rsqrt(jnp.mean(values * values, axis=-1, keepdims=True) + EPS) * gains


def inner_rows(left, right):
    return lax.dot_general(
        left, right, (((0,), (0,)), ((), ())), preferred_element_type=jnp.float32
    )


def times_trans(left, right):
    return lax.dot_general(
        left, right, (((1,), (1,)), ((), ())), preferred_element_type=jnp.float32
    )


def split_blocks(whole):
    length = whole.shape[0]
    width = min(512, length)
    count = length // width
    return (whole.reshape(count, width, HEADS, HDIM), width, count)


def block_at(blocks, index):
    return lax.dynamic_index_in_dim(blocks, index, 0, keepdims=False)


def key_scores(query, key_block, key_start, query_pos):
    scale = HDIM ** (-0.5)
    scores = (
        jnp.einsum("qhd,khd->hqk", query, key_block, preferred_element_type=jnp.float32) * scale
    )
    key_pos = key_start + jnp.arange(key_block.shape[0], dtype=jnp.int32)
    allowed = key_pos[None, :] <= query_pos[:, None]
    return (scores, allowed[None])


def attend(query, keys_all, values_all, query_pos):
    key_blocks, width, count = split_blocks(keys_all)
    value_blocks = split_blocks(values_all)[0]
    row_count = query.shape[0]
    upper = query_pos[row_count - 1] // width + 1

    def total_step(index, carry):
        running, total = carry
        scores, allowed = key_scores(query, block_at(key_blocks, index), index * width, query_pos)
        newest = jnp.maximum(running, jnp.max(jnp.where(allowed, scores, NEGATIVE), axis=-1))
        terms = jnp.where(allowed, jnp.exp(scores - newest[..., None]), 0.0)
        total = total * jnp.exp(running - newest) + jnp.sum(terms, axis=-1)
        return (newest, total)

    start_run = jnp.full((HEADS, row_count), NEGATIVE, jnp.float32)
    start_total = jnp.zeros((HEADS, row_count), jnp.float32)
    running, total = lax.fori_loop(0, upper, total_step, (start_run, start_total))
    log_total = running + jnp.log(total)

    def mix_step(index, accum):
        scores, allowed = key_scores(query, block_at(key_blocks, index), index * width, query_pos)
        probs = jnp.where(allowed, jnp.exp(scores - log_total[..., None]), 0.0)
        return accum + jnp.einsum(
            "hqk,khd->qhd",
            probs.astype(jnp.bfloat16),
            block_at(value_blocks, index),
            preferred_element_type=jnp.float32,
        )

    start_mix = jnp.zeros((row_count, HEADS, HDIM), jnp.float32)
    mixed = lax.fori_loop(0, upper, mix_step, start_mix)
    return (mixed.reshape(row_count, HEADS * HDIM), log_total)


def attend_back(query, keys_all, values_all, log_total, out_grad, delta, query_pos):
    key_blocks, width, count = split_blocks(keys_all)
    value_blocks = split_blocks(values_all)[0]
    row_count = query.shape[0]
    upper = query_pos[row_count - 1] // width + 1
    scale = HDIM ** (-0.5)

    def back_step(index, carry):
        query_acc, pieces = carry
        key_block = block_at(key_blocks, index)
        value_block = block_at(value_blocks, index)
        scores, allowed = key_scores(query, key_block, index * width, query_pos)
        probs = jnp.where(allowed, jnp.exp(scores - log_total[..., None]), 0.0)
        prob_grad = jnp.einsum(
            "qhd,khd->hqk", out_grad, value_block, preferred_element_type=jnp.float32
        )
        score_grad = (probs * (prob_grad - delta[..., None])).astype(jnp.bfloat16)
        query_acc = (
            query_acc
            + jnp.einsum("hqk,khd->qhd", score_grad, key_block, preferred_element_type=jnp.float32)
            * scale
        )
        key_grad = (
            jnp.einsum("hqk,qhd->khd", score_grad, query, preferred_element_type=jnp.float32)
            * scale
        )
        value_grad = jnp.einsum(
            "hqk,qhd->khd", probs.astype(jnp.bfloat16), out_grad, preferred_element_type=jnp.float32
        )
        joined = jnp.concatenate(
            [key_grad.reshape(width, HEADS * HDIM), value_grad.reshape(width, HEADS * HDIM)], axis=1
        )
        pieces = lax.dynamic_update_index_in_dim(pieces, joined, index, 0)
        return (query_acc, pieces)

    start_acc = jnp.zeros((row_count, HEADS, HDIM), jnp.float32)
    start_pieces = jnp.zeros((count, width, 2 * HEADS * HDIM), jnp.float32)
    query_grad, pieces = lax.fori_loop(0, upper, back_step, (start_acc, start_pieces))
    return (query_grad.reshape(row_count, HEADS * HDIM), pieces.reshape(-1, pieces.shape[-1]))


def layer_forward(hidden_in, weights, query_pos):
    w_qkv_full, w_out_full, w_up_full, w_down_full, gain_full = weights
    gains_f = gain_full.astype(jnp.float32)
    row_count = hidden_in.shape[0]
    width = w_out_full.shape[1]
    normed = norm_apply(hidden_in, gains_f[:, 0]).astype(jnp.bfloat16)
    qkv_low = jnp.dot(normed, w_qkv_full, preferred_element_type=jnp.float32).astype(jnp.bfloat16)
    query = qkv_low[:, :width]
    keys_all, values_all = (
        lax.all_gather(qkv_low[:, width : 2 * width], "grp", axis=0, tiled=True),
        lax.all_gather(qkv_low[:, 2 * width :], "grp", axis=0, tiled=True),
    )
    mixed, log_total = attend(
        query.reshape(row_count, HEADS, HDIM),
        keys_all.reshape(-1, HEADS, HDIM),
        values_all.reshape(-1, HEADS, HDIM),
        query_pos,
    )
    mixed_low = mixed.astype(jnp.bfloat16)
    attn_out = jnp.dot(mixed_low, w_out_full, preferred_element_type=jnp.float32)
    resid = hidden_in + norm_apply(attn_out, gains_f[:, 1])
    mlp_in = norm_apply(resid, gains_f[:, 2]).astype(jnp.bfloat16)
    up_out = jnp.dot(mlp_in, w_up_full, preferred_element_type=jnp.float32)
    active = jax.nn.gelu(up_out).astype(jnp.bfloat16)
    down_out = jnp.dot(active, w_down_full, preferred_element_type=jnp.float32)
    result = resid + norm_apply(down_out, gains_f[:, 3])
    kept = (
        hidden_in,
        normed,
        qkv_low,
        mixed,
        mixed_low,
        log_total,
        attn_out,
        resid,
        mlp_in,
        up_out,
        active,
        down_out,
    )
    return (result, kept)


def layer_backward(grad_out, weights, kept, query_pos):
    w_qkv_full, w_out_full, w_up_full, w_down_full, gain_full = weights
    (
        hidden_in,
        normed,
        qkv_low,
        mixed,
        mixed_low,
        log_total,
        attn_out,
        resid,
        mlp_in,
        up_out,
        active,
        down_out,
    ) = kept
    gains_f = gain_full.astype(jnp.float32)
    row_count = hidden_in.shape[0]
    width = w_out_full.shape[1]
    unused, puller = jax.vjp(norm_apply, down_out, gains_f[:, 3])
    down_grad, gain_four = puller(grad_out)
    down_low = down_grad.astype(jnp.bfloat16)
    w_down_grad = inner_rows(active, down_low)
    active_grad = times_trans(down_low, w_down_full)
    unused, puller = jax.vjp(jax.nn.gelu, up_out)
    up_low = puller(active_grad)[0].astype(jnp.bfloat16)
    w_up_grad = inner_rows(mlp_in, up_low)
    mlp_grad = times_trans(up_low, w_up_full)
    unused, puller = jax.vjp(norm_apply, resid, gains_f[:, 2])
    resid_part, gain_three = puller(mlp_grad)
    resid_grad = grad_out + resid_part
    unused, puller = jax.vjp(norm_apply, attn_out, gains_f[:, 1])
    attn_grad, gain_two = puller(resid_grad)
    attn_low = attn_grad.astype(jnp.bfloat16)
    w_out_grad = inner_rows(mixed_low, attn_low)
    mixed_grad = times_trans(attn_low, w_out_full).astype(jnp.bfloat16)
    keys_all, values_all = (
        lax.all_gather(qkv_low[:, width : 2 * width], "grp", axis=0, tiled=True),
        lax.all_gather(qkv_low[:, 2 * width :], "grp", axis=0, tiled=True),
    )
    delta = jnp.sum(
        (mixed_grad.astype(jnp.float32) * mixed).reshape(row_count, HEADS, HDIM), axis=-1
    ).T
    query_low = qkv_low[:, :width]
    query_grad, key_value_terms = attend_back(
        query_low.reshape(row_count, HEADS, HDIM),
        keys_all.reshape(-1, HEADS, HDIM),
        values_all.reshape(-1, HEADS, HDIM),
        log_total,
        mixed_grad.reshape(row_count, HEADS, HDIM),
        delta,
        query_pos,
    )
    key_value_grad = lax.psum_scatter(
        key_value_terms.astype(jnp.bfloat16), "grp", scatter_dimension=0, tiled=True
    ).astype(jnp.float32)
    qkv_grad = jnp.concatenate([query_grad, key_value_grad], axis=1).astype(jnp.bfloat16)
    w_qkv_grad = inner_rows(normed, qkv_grad)
    normed_grad = times_trans(qkv_grad, w_qkv_full)
    unused, puller = jax.vjp(norm_apply, hidden_in, gains_f[:, 0])
    input_part, gain_one = puller(normed_grad)
    gain_grad = jnp.stack([gain_one, gain_two, gain_three, gain_four], axis=1)
    return (resid_grad + input_part, (w_qkv_grad, w_out_grad, w_up_grad, w_down_grad, gain_grad))


def body(block_in, cotangent, w_qkv, w_out, w_up, w_down, norm_gains):
    layer_count = w_qkv.shape[0]
    micro_count = block_in.shape[0]
    row_count = block_in.shape[2]
    query_pos = lax.axis_index("grp") * row_count + jnp.arange(row_count, dtype=jnp.int32)
    totals = [None] * layer_count
    outputs = []
    input_grads = []
    for micro_idx in range(micro_count):
        hidden = block_in[micro_idx, 0].astype(jnp.float32)
        saved = []
        for layer_idx in range(layer_count):
            hidden, kept = layer_forward(
                hidden,
                (
                    lax.all_gather(w_qkv[layer_idx], "grp", axis=0, tiled=True),
                    lax.all_gather(w_out[layer_idx], "grp", axis=0, tiled=True),
                    lax.all_gather(w_up[layer_idx], "grp", axis=0, tiled=True),
                    lax.all_gather(w_down[layer_idx], "grp", axis=0, tiled=True),
                    lax.all_gather(norm_gains[layer_idx], "grp", axis=0, tiled=True),
                ),
                query_pos,
            )
            saved.append(kept)
        outputs.append(hidden.astype(jnp.bfloat16))
        grad_flow = cotangent[micro_idx, 0].astype(jnp.float32)
        for layer_idx in reversed(range(layer_count)):
            grad_flow, parts = layer_backward(
                grad_flow,
                (
                    lax.all_gather(w_qkv[layer_idx], "grp", axis=0, tiled=True),
                    lax.all_gather(w_out[layer_idx], "grp", axis=0, tiled=True),
                    lax.all_gather(w_up[layer_idx], "grp", axis=0, tiled=True),
                    lax.all_gather(w_down[layer_idx], "grp", axis=0, tiled=True),
                    lax.all_gather(norm_gains[layer_idx], "grp", axis=0, tiled=True),
                ),
                saved[layer_idx],
                query_pos,
            )
            if totals[layer_idx] is None:
                totals[layer_idx] = parts
            else:
                totals[layer_idx] = tuple(
                    (left + right for left, right in zip(totals[layer_idx], parts))
                )
        input_grads.append(grad_flow)
    reduced = []
    for layer_idx in range(layer_count):
        accum = totals[layer_idx]
        shards = (
            lax.psum_scatter(
                accum[0].astype(jnp.bfloat16), "grp", scatter_dimension=0, tiled=True
            ).astype(jnp.float32),
            lax.psum_scatter(
                accum[1].astype(jnp.bfloat16), "grp", scatter_dimension=0, tiled=True
            ).astype(jnp.float32),
            lax.psum_scatter(
                accum[2].astype(jnp.bfloat16), "grp", scatter_dimension=0, tiled=True
            ).astype(jnp.float32),
            lax.psum_scatter(
                accum[3].astype(jnp.bfloat16), "grp", scatter_dimension=0, tiled=True
            ).astype(jnp.float32),
            lax.psum_scatter(
                accum[4].astype(jnp.bfloat16), "grp", scatter_dimension=0, tiled=True
            ).astype(jnp.float32),
        )
        reduced.append(
            (
                lax.psum(shards[0].astype(jnp.bfloat16), "rep").astype(jnp.float32),
                lax.psum(shards[1].astype(jnp.bfloat16), "rep").astype(jnp.float32),
                lax.psum(shards[2].astype(jnp.bfloat16), "rep").astype(jnp.float32),
                lax.psum(shards[3].astype(jnp.bfloat16), "rep").astype(jnp.float32),
                lax.psum(shards[4].astype(jnp.bfloat16), "rep").astype(jnp.float32),
            )
        )
    block_out = jnp.stack(outputs)[:, None]
    block_in_grad = jnp.stack(input_grads)[:, None]
    stacked = [
        jnp.stack([reduced[layer_idx][member] for layer_idx in range(layer_count)])
        for member in range(5)
    ]
    return (block_out, block_in_grad, stacked[0], stacked[1], stacked[2], stacked[3], stacked[4])


def solution(mesh):
    return jax.shard_map(
        body,
        mesh=mesh,
        in_specs=(
            P(None, "rep", "grp", None),
            P(None, "rep", "grp", None),
            P(None, "grp", None),
            P(None, "grp", None),
            P(None, "grp", None),
            P(None, "grp", None),
            P(None, "grp", None),
        ),
        out_specs=(
            P(None, "rep", "grp", None),
            P(None, "rep", "grp", None),
            P(None, "grp", None),
            P(None, "grp", None),
            P(None, "grp", None),
            P(None, "grp", None),
            P(None, "grp", None),
        ),
        check_vma=False,
    )
```

profile of v0, /device:TPU:0, one launch (start us, length us, event | category | flops | bytes accessed | tf_op | source)
XLA Modules:
  0.0 1937.6 jit_solution(5514778637835726931)
XLA Ops:
  10.0 13.4 all-gather
  23.7 54.0 %all-gather.43.cloned.1.call-done = bf16[1,1024,3072]{2,1,0:T(8,128)(2,1)} async-done(((bf16[1,128,3072]{2,1,0:T(8,128)(2,1)}), bf16[1,1024,3072]{2,1,0:T(8,128)(2,1)}) %all-gather.43.cloned.1.call-update) | async-done | bytes 6291472 | tf_op jit(solution)/shard_map/all_gather | solution.py:247
  98.6 9.1 all-gather.5
  110.4 6.3 reshape.879
  123.4 17.8 all-gather.35.cloned.1.call-done
  156.6 15.3 all-gather.45.cloned.1.call-done
  174.8 27.8 %all-gather.29.cloned.1.call-done = bf16[1024,1024]{1,0:T(8,128)(2,1)} async-done(((bf16[128,1024]{1,0:T(8,128)(2,1)}), bf16[1024,1024]{1,0:T(8,128)(2,1)}) %all-gather.29.cloned.1.call-update) | async-done | bytes 2097168 | tf_op jit(solution)/shard_map/all_gather | solution.py:133
  214.5 18.2 all-gather.27.cloned.1.call-done
  255.1 60.7 %all-gather.47.cloned.1.call-done = bf16[1,1024,4096]{2,1,0:T(8,128)(2,1)} async-done(((bf16[1,128,4096]{2,1,0:T(8,128)(2,1)}), bf16[1,1024,4096]{2,1,0:T(8,128)(2,1)}) %all-gather.47.cloned.1.call-update) | async-done | bytes 8388624 | tf_op jit(solution)/shard_map/all_gather | solution.py:249
  320.6 78.0 %all-gather.49.cloned.1.call-done = bf16[1,4096,1024]{2,1,0:T(8,128)(2,1)} async-done(((bf16[1,512,1024]{2,1,0:T(8,128)(2,1)}), bf16[1,4096,1024]{2,1,0:T(8,128)(2,1)}) %all-gather.49.cloned.1.call-update) | async-done | bytes 8388624 | tf_op jit(solution)/shard_map/all_gather | solution.py:250
  413.7 49.9 %all-gather.51.cloned.1.call-done = bf16[1,1024,3072]{2,1,0:T(8,128)(2,1)} async-done(((bf16[1,128,3072]{2,1,0:T(8,128)(2,1)}), bf16[1,1024,3072]{2,1,0:T(8,128)(2,1)}) %all-gather.51.cloned.1.call-update) | async-done | bytes 6291472 | tf_op jit(solution)/shard_map/all_gather | solution.py:247
  477.1 19.1 all-gather.33.cloned.1.call-done
  509.4 17.1 all-gather.41.cloned.1.call-done
  526.5 6.3 reshape.881
  538.4 18.2 all-gather.39.cloned.1.call-done
  568.6 18.9 all-gather.31.cloned.1.call-done
  622.5 78.0 %all-gather.55.cloned.1.call-done = bf16[1,1024,4096]{2,1,0:T(8,128)(2,1)} async-done(((bf16[1,128,4096]{2,1,0:T(8,128)(2,1)}), bf16[1,1024,4096]{2,1,0:T(8,128)(2,1)}) %all-gather.55.cloned.1.call-update) | async-done | bytes 8388624 | tf_op jit(solution)/shard_map/all_gather | solution.py:249
  706.6 76.6 %all-gather.57.cloned.1.call-done = bf16[1,4096,1024]{2,1,0:T(8,128)(2,1)} async-done(((bf16[1,512,1024]{2,1,0:T(8,128)(2,1)}), bf16[1,4096,1024]{2,1,0:T(8,128)(2,1)}) %all-gather.57.cloned.1.call-update) | async-done | bytes 8388624 | tf_op jit(solution)/shard_map/all_gather | solution.py:250
  799.4 7.1 fusion.273
  806.5 7.5 fusion.287
  836.6 17.2 while.158
  857.3 18.7 while.156
  879.6 39.9 %reduce-scatter.23.cloned.1.call-done = bf16[128,2048]{1,0:T(8,128)(2,1)} async-done(((bf16[1024,2048]{1,0:T(8,128)(2,1)}), bf16[128,2048]{1,0:T(8,128)(2,1)}) %reduce-scatter.23.cloned.1.call-update) | async-done | bytes 524304 | tf_op jit(solution)/shard_map/reduce_scatter | solution.py:220
  925.6 44.9 %reduce-scatter.19.cloned.1.call-done = bf16[128,2048]{1,0:T(8,128)(2,1)} async-done(((bf16[1024,2048]{1,0:T(8,128)(2,1)}), bf16[128,2048]{1,0:T(8,128)(2,1)}) %reduce-scatter.19.cloned.1.call-update) | async-done | bytes 524304 | tf_op jit(solution)/shard_map/reduce_scatter | solution.py:220
  979.7 7.1 fusion.266
  1005.5 17.1 while.157
  1031.6 17.4 while.159
  1058.4 9.3 fusion.407
  1067.7 9.7 add_convert_fusion
  1078.5 9.5 fusion.405
  1088.0 11.5 add_convert_fusion.2
  1109.8 9.3 fusion.406
  1119.1 9.6 add_convert_fusion.1
  1129.7 9.5 fusion.404
  1139.3 11.5 add_convert_fusion.3
  1151.9 7.5 fusion.360
  1159.4 9.4 add_convert_fusion.5
  1181.9 30.3 %reduce-scatter.31.cloned.1.call-done = bf16[128,1024]{1,0:T(8,128)(2,1)} async-done(((bf16[1024,1024]{1,0:T(8,128)(2,1)}), bf16[128,1024]{1,0:T(8,128)(2,1)}) %reduce-scatter.31.cloned.1.call-update) | async-done | bytes 262160 | tf_op jit(solution)/shard_map/reduce_scatter | solution.py:285
  1212.2 90.7 %reduce-scatter.41.cloned.1.call-done = bf16[512,1024]{1,0:T(8,128)(2,1)} async-done(((bf16[4096,1024]{1,0:T(8,128)(2,1)}), bf16[512,1024]{1,0:T(8,128)(2,1)}) %reduce-scatter.41.cloned.1.call-update) | async-done | bytes 1048592 | tf_op jit(solution)/shard_map/reduce_scatter | solution.py:291
  1302.9 90.1 %reduce-scatter.37.cloned.1.call-done = bf16[128,4096]{1,0:T(8,128)(2,1)} async-done(((bf16[1024,4096]{1,0:T(8,128)(2,1)}), bf16[128,4096]{1,0:T(8,128)(2,1)}) %reduce-scatter.37.cloned.1.call-update) | async-done | bytes 1048592 | tf_op jit(solution)/shard_map/reduce_scatter | solution.py:288
  1393.0 70.5 %reduce-scatter.29.cloned.1.call-done = bf16[128,3072]{1,0:T(8,128)(2,1)} async-done(((bf16[1024,3072]{1,0:T(8,128)(2,1)}), bf16[128,3072]{1,0:T(8,128)(2,1)}) %reduce-scatter.29.cloned.1.call-update) | async-done | bytes 786448 | tf_op jit(solution)/shard_map/reduce_scatter | solution.py:282
  1463.5 90.2 %reduce-scatter.39.cloned.1.call-done = bf16[512,1024]{1,0:T(8,128)(2,1)} async-done(((bf16[4096,1024]{1,0:T(8,128)(2,1)}), bf16[512,1024]{1,0:T(8,128)(2,1)}) %reduce-scatter.39.cloned.1.call-update) | async-done | bytes 1048592 | tf_op jit(solution)/shard_map/reduce_scatter | solution.py:291
  1553.7 90.1 %reduce-scatter.35.cloned.1.call-done = bf16[128,4096]{1,0:T(8,128)(2,1)} async-done(((bf16[1024,4096]{1,0:T(8,128)(2,1)}), bf16[128,4096]{1,0:T(8,128)(2,1)}) %reduce-scatter.35.cloned.1.call-update) | async-done | bytes 1048592 | tf_op jit(solution)/shard_map/reduce_scatter | solution.py:288
  1643.8 70.5 %reduce-scatter.27.cloned.1.call-done = bf16[128,3072]{1,0:T(8,128)(2,1)} async-done(((bf16[1024,3072]{1,0:T(8,128)(2,1)}), bf16[128,3072]{1,0:T(8,128)(2,1)}) %reduce-scatter.27.cloned.1.call-update) | async-done | bytes 786448 | tf_op jit(solution)/shard_map/reduce_scatter | solution.py:282
  1716.2 29.7 %reduce-scatter.45.cloned.1.call-done = bf16[128,4]{1,0:T(8,128)(2,1)} async-done(((bf16[1024,4]{1,0:T(8,128)(2,1)}), bf16[128,4]{1,0:T(8,128)(2,1)}) %reduce-scatter.45.cloned.1.call-update) | async-done | bytes 1040
  1748.1 29.0 %reduce-scatter.43.cloned.1.call-done = bf16[128,4]{1,0:T(8,128)(2,1)} async-done(((bf16[1024,4]{1,0:T(8,128)(2,1)}), bf16[128,4]{1,0:T(8,128)(2,1)}) %reduce-scatter.43.cloned.1.call-update) | async-done | bytes 1040
  1777.9 9.9 all-reduce
  1788.4 132.3 %all-reduce.4.cloned.1.call-done = (bf16[1,128,3072]{2,1,0:T(8,128)(2,1)}, bf16[1,128,3072]{2,1,0:T(8,128)(2,1)}, bf16[1,128,1024]{2,1,0:T(8,128)(2,1)}, bf16[1,...) async-done(((bf16[1,128,3072]{2,1,0:T(8,128)(2,1)}, ...) | async-done | bytes 6291472 | tf_op jit(solution)/shard_map/psum | solution.py:300
  (801 shorter events, 416.1 us)
Async XLA Ops:
  7.2 70.5 %all-gather.43.cloned.1.call-start = ((), (), s32[]{:S(2)}) async-start(), calls=%async_computation.34 | async-start | bytes 7077888 | tf_op jit(solution)/shard_map/all_gather | solution.py:247
  9.9 100.5 %all-gather.37.cloned.1.call-start = ((), (), s32[]{:S(2)}) async-start(), calls=%async_computation.19 | async-start | bytes 2359296 | tf_op jit(solution)/shard_map/all_gather | solution.py:133
  23.7 230.2 %copy-start.148 = (f32[1024,1]{0,1:T(1,128)}, f32[1024,1]{0,1:T(1,128)S(1)}, u32[]{:S(2)}) copy-start(f32[1024,1]{0,1:T(1,128)S(1)} %get-tuple-element.1612) | copy-start | bytes 12292
  23.7 380.5 %copy-start.129 = (f32[1024,1]{0,1:T(1,128)}, f32[1024,1]{0,1:T(1,128)S(1)}, u32[]{:S(2)}) copy-start(f32[1024,1]{0,1:T(1,128)S(1)} %get-tuple-element.1610) | copy-start | bytes 12292
  23.7 389.6 %copy-start.150 = (f32[1024,1]{0,1:T(1,128)}, f32[1024,1]{0,1:T(1,128)S(1)}, u32[]{:S(2)}) copy-start(f32[1024,1]{0,1:T(1,128)S(1)} %get-tuple-element.1611) | copy-start | bytes 12292
  82.5 58.8 %all-gather.35.cloned.1.call-start = ((), (), s32[]{:S(2)}) async-start(), calls=%async_computation.18 | async-start | bytes 2359296 | tf_op jit(solution)/shard_map/all_gather | solution.py:134
  83.2 88.7 %all-gather.45.cloned.1.call-start = ((), (), s32[]{:S(2)}) async-start(), calls=%async_computation.35 | async-start | bytes 2359296 | tf_op jit(solution)/shard_map/all_gather | solution.py:248
  84.1 118.5 %all-gather.29.cloned.1.call-start = ((), (), s32[]{:S(2)}) async-start(), calls=%async_computation.15 | async-start | bytes 2359296 | tf_op jit(solution)/shard_map/all_gather | solution.py:133
  89.0 143.7 %all-gather.27.cloned.1.call-start = ((), (), s32[]{:S(2)}) async-start(), calls=%async_computation.14 | async-start | bytes 2359296 | tf_op jit(solution)/shard_map/all_gather | solution.py:134
  89.5 226.3 %all-gather.47.cloned.1.call-start = ((), (), s32[]{:S(2)}) async-start(), calls=%async_computation.36 | async-start | bytes 9437184 | tf_op jit(solution)/shard_map/all_gather | solution.py:249
  91.5 307.1 %all-gather.49.cloned.1.call-start = ((), (), s32[]{:S(2)}) async-start(), calls=%async_computation.37 | async-start | bytes 9437184 | tf_op jit(solution)/shard_map/all_gather | solution.py:250
  94.6 369.0 %all-gather.51.cloned.1.call-start = ((), (), s32[]{:S(2)}) async-start(), calls=%async_computation.38 | async-start | bytes 7077888 | tf_op jit(solution)/shard_map/all_gather | solution.py:247
  95.4 400.9 %all-gather.33.cloned.1.call-start = ((), (), s32[]{:S(2)}) async-start(), calls=%async_computation.17 | async-start | bytes 2359296 | tf_op jit(solution)/shard_map/all_gather | solution.py:133
  108.4 360.0 %copy-start.140 = (f32[1024,1]{0,1:T(1,128)}, f32[1024,1]{0,1:T(1,128)S(1)}, u32[]{:S(2)}) copy-start(f32[1024,1]{0,1:T(1,128)S(1)} %get-tuple-element.1609) | copy-start | bytes 12292
  255.1 149.1 %copy-start.205 = (f32[128]{0:T(128)}, f32[128]{0:T(128)S(1)}, u32[]{:S(2)}) copy-start(f32[128]{0:T(128)S(1)} %get-tuple-element.1557) | copy-start | bytes 1540
  255.1 158.2 %copy-start.32 = (f32[128,1024]{1,0:T(8,128)}, f32[128,1024]{1,0:T(8,128)S(1)}, u32[]{:S(2)}) copy-start(f32[128,1024]{1,0:T(8,128)S(1)} %get-tuple-element.1603) | copy-start | bytes 1572868
  320.6 83.1 %copy-start.72 = (f32[128,4096]{1,0:T(8,128)}, f32[128,4096]{1,0:T(8,128)S(1)}, u32[]{:S(2)}) copy-start(f32[128,4096]{1,0:T(8,128)S(1)} %fusion.228) | copy-start | bytes 6291460
  320.6 83.6 %copy-start.35 = (f32[128,1024]{1,0:T(8,128)S(1)}, f32[128,1024]{1,0:T(8,128)}, u32[]{:S(2)}) copy-start(f32[128,1024]{1,0:T(8,128)} %get-tuple-element.1558) | copy-start | bytes 1572868
  468.3 58.2 %all-gather.41.cloned.1.call-start = ((), (), s32[]{:S(2)}) async-start(), calls=%async_computation.21 | async-start | bytes 2359296 | tf_op jit(solution)/shard_map/all_gather | solution.py:133
  473.6 83.0 %all-gather.39.cloned.1.call-start = ((), (), s32[]{:S(2)}) async-start(), calls=%async_computation.20 | async-start | bytes 2359296 | tf_op jit(solution)/shard_map/all_gather | solution.py:134
  474.2 113.2 %all-gather.31.cloned.1.call-start = ((), (), s32[]{:S(2)}) async-start(), calls=%async_computation.16 | async-start | bytes 2359296 | tf_op jit(solution)/shard_map/all_gather | solution.py:134
  475.0 142.5 %all-gather.53.cloned.1.call-start = ((), (), s32[]{:S(2)}) async-start(), calls=%async_computation.39 | async-start | bytes 2359296 | tf_op jit(solution)/shard_map/all_gather | solution.py:248
  475.5 225.0 %all-gather.55.cloned.1.call-start = ((), (), s32[]{:S(2)}) async-start(), calls=%async_computation.40 | async-start | bytes 9437184 | tf_op jit(solution)/shard_map/all_gather | solution.py:249
  476.1 307.1 %all-gather.57.cloned.1.call-start = ((), (), s32[]{:S(2)}) async-start(), calls=%async_computation.41 | async-start | bytes 9437184 | tf_op jit(solution)/shard_map/all_gather | solution.py:250
  476.7 442.8 %reduce-scatter.23.cloned.1.call-start = ((), (), s32[]{:S(2)}) async-start(), calls=%async_computation.24 | async-start | bytes 4718592 | tf_op jit(solution)/shard_map/reduce_scatter | solution.py:220
  620.6 79.9 %copy-start.132 = (f32[1024,1]{0,1:T(1,128)S(1)}, f32[1024,1]{0,1:T(1,128)}, u32[]{:S(2)}) copy-start(f32[1024,1]{0,1:T(1,128)} %get-tuple-element.1607) | copy-start | bytes 12292
  622.5 198.1 %copy-start.38 = (f32[128,1024]{1,0:T(8,128)}, f32[128,1024]{1,0:T(8,128)S(1)}, u32[]{:S(2)}) copy-start(f32[128,1024]{1,0:T(8,128)S(1)} %get-tuple-element.1633) | copy-start | bytes 1572868
  622.5 198.1 %copy-start.176 = (f32[128]{0:T(128)}, f32[128]{0:T(128)S(1)}, u32[]{:S(2)}) copy-start(f32[128]{0:T(128)S(1)} %fusion.394) | copy-start | bytes 1540
  853.9 116.5 %reduce-scatter.19.cloned.1.call-start = ((), (), s32[]{:S(2)}) async-start(), calls=%async_computation.22 | async-start | bytes 4718592 | tf_op jit(solution)/shard_map/reduce_scatter | solution.py:220
  876.1 275.2 %reduce-scatter.21.cloned.1.call-start = ((), (), s32[]{:S(2)}) async-start(), calls=%async_computation.23 | async-start | bytes 4718592 | tf_op jit(solution)/shard_map/reduce_scatter | solution.py:220
  879.3 91.1 %copy-start.111 = (bf16[128,1024]{1,0:T(8,128)(2,1)}, bf16[128,1024]{1,0:T(8,128)(2,1)S(1)}, u32[]{:S(2)}) copy-start(bf16[128,1024]{1,0:T(8,128)(2,1)S(1)} %copy.250) | copy-start | bytes 786436
  879.5 90.9 %copy-start.44 = (f32[128,1024]{1,0:T(8,128)S(1)}, f32[128,1024]{1,0:T(8,128)}, u32[]{:S(2)}) copy-start(f32[128,1024]{1,0:T(8,128)} %copy-done.42) | copy-start | bytes 1572868
  879.5 90.9 %copy-start.48 = (f32[128,1024]{1,0:T(8,128)S(1)}, f32[128,1024]{1,0:T(8,128)}, u32[]{:S(2)}) copy-start(f32[128,1024]{1,0:T(8,128)} %copy-done.46) | copy-start | bytes 1572868
  879.5 90.9 %copy-start.141 = (f32[1024,1]{0,1:T(1,128)S(1)}, f32[1024,1]{0,1:T(1,128)}, u32[]{:S(2)}) copy-start(f32[1024,1]{0,1:T(1,128)} %copy-done.140) | copy-start | bytes 12292
  879.6 90.9 %copy-start.179 = (f32[128]{0:T(128)S(1)}, f32[128]{0:T(128)}, u32[]{:S(2)}) copy-start(f32[128]{0:T(128)} %copy-done.178) | copy-start | bytes 1540
  879.6 90.9 %copy-start.184 = (f32[128]{0:T(128)S(1)}, f32[128]{0:T(128)}, u32[]{:S(2)}) copy-start(f32[128]{0:T(128)} %copy-done.183) | copy-start | bytes 1540
  1022.6 136.8 %reduce-scatter.25.cloned.1.call-start = ((), (), s32[]{:S(2)}) async-start(), calls=%async_computation.25 | async-start | bytes 4718592 | tf_op jit(solution)/shard_map/reduce_scatter | solution.py:220
  1049.1 132.8 %reduce-scatter.33.cloned.1.call-start = ((), (), s32[]{:S(2)}) async-start(), calls=%async_computation.29 | async-start | bytes 2359296 | tf_op jit(solution)/shard_map/reduce_scatter | solution.py:285
  1052.9 159.3 %reduce-scatter.31.cloned.1.call-start = ((), (), s32[]{:S(2)}) async-start(), calls=%async_computation.28 | async-start | bytes 2359296 | tf_op jit(solution)/shard_map/reduce_scatter | solution.py:285
  1056.8 246.1 %reduce-scatter.41.cloned.1.call-start = ((), (), s32[]{:S(2)}) async-start(), calls=%async_computation.33 | async-start | bytes 9437184 | tf_op jit(solution)/shard_map/reduce_scatter | solution.py:291
  1077.5 315.6 %reduce-scatter.37.cloned.1.call-start = ((), (), s32[]{:S(2)}) async-start(), calls=%async_computation.31 | async-start | bytes 9437184 | tf_op jit(solution)/shard_map/reduce_scatter | solution.py:288
  1099.5 364.0 %reduce-scatter.29.cloned.1.call-start = ((), (), s32[]{:S(2)}) async-start(), calls=%async_computation.27 | async-start | bytes 7077888 | tf_op jit(solution)/shard_map/reduce_scatter | solution.py:282
  1108.2 445.5 %reduce-scatter.39.cloned.1.call-start = ((), (), s32[]{:S(2)}) async-start(), calls=%async_computation.32 | async-start | bytes 9437184 | tf_op jit(solution)/shard_map/reduce_scatter | solution.py:291
  1128.7 515.1 %reduce-scatter.35.cloned.1.call-start = ((), (), s32[]{:S(2)}) async-start(), calls=%async_computation.30 | async-start | bytes 9437184 | tf_op jit(solution)/shard_map/reduce_scatter | solution.py:288
  1150.8 563.5 %reduce-scatter.27.cloned.1.call-start = ((), (), s32[]{:S(2)}) async-start(), calls=%async_computation.26 | async-start | bytes 7077888 | tf_op jit(solution)/shard_map/reduce_scatter | solution.py:282
  1168.9 577.0 %reduce-scatter.45.cloned.1.call-start = ((), (), s32[]{:S(2)}) async-start(), calls=%async_computation.43 | async-start | bytes 294912
  1170.5 606.6 %reduce-scatter.43.cloned.1.call-start = ((), (), s32[]{:S(2)}) async-start(), calls=%async_computation.42 | async-start | bytes 294912
  1181.8 738.9 %all-reduce.4.cloned.1.call-start = ((), (), s32[]{:S(2)}) async-start(), calls=%async_computation.44 | async-start | bytes 12582912 | tf_op jit(solution)/shard_map/psum | solution.py:300
  (212 other events, 2450.5 us)
Sparse Core Ops, SparseCore 0:
  10.2 67.4 all-gather.42
  82.6 27.8 all-gather.36
  112.6 28.5 all-gather.34
  143.3 28.5 all-gather.44
  174.0 28.5 all-gather.28
  204.0 28.5 all-gather.26
  234.3 81.5 all-gather.46
  318.0 80.5 all-gather.48
  400.3 63.2 all-gather.50
  468.4 27.7 all-gather.32
  497.8 28.6 all-gather.40
  528.0 28.5 all-gather.38
  558.8 28.6 all-gather.30
  588.9 28.5 all-gather.52
  618.9 81.5 all-gather.54
  702.6 80.5 all-gather.56
  854.0 65.4 reduce-scatter.22
  922.2 48.1 reduce-scatter.18
  1022.7 64.9 reduce-scatter.20
  1090.4 48.1 reduce-scatter.24
  1141.5 33.9 reduce-scatter.32
  1177.7 34.4 reduce-scatter.30
  1214.5 88.3 reduce-scatter.40
  1305.0 87.9 reduce-scatter.36
  1395.3 68.1 reduce-scatter.28
  1465.7 87.9 reduce-scatter.38
  1555.8 87.9 reduce-scatter.34
  1646.1 68.1 reduce-scatter.26
  1717.1 28.6 reduce-scatter.44
  1748.6 28.4 reduce-scatter.42
  1781.5 139.1 all-reduce.3
where the time goes:
time: 1950 us; the launch traced here: 1940 us
  waiting for transfers between devices  1370 us (70%)
  matrix products  293 us (15%)
  local copies, waits for them, and re-layouts  187 us (10%)
  blocking collectives  32.5 us (2%)
  other arithmetic  28.8 us (1%)
  between operations  20.1 us (1%)
    reduce_scatter x2, waiting for transfers between devices, body(): lax.psum_scatter(accum[3].astype(jnp.bfloat16), 'grp', scatter_dimension=...  181 us
    reduce_scatter x2, waiting for transfers between devices, body(): lax.psum_scatter(accum[2].astype(jnp.bfloat16), 'grp', scatter_dimension=...  180 us
    all_gather x2, waiting for transfers between devices, body(): lax.all_gather(w_down[layer_idx], 'grp', axis=0, tiled=True)  155 us
    reduce_scatter x2, waiting for transfers between devices, body(): lax.psum_scatter(accum[0].astype(jnp.bfloat16), 'grp', scatter_dimension=...  141 us
    all_gather x2, waiting for transfers between devices, body(): lax.all_gather(w_up[layer_idx], 'grp', axis=0, tiled=True)  139 us
    psum x1, waiting for transfers between devices, body(): lax.psum(shards[0].astype(jnp.bfloat16), 'rep').astype(jnp.float32)  132 us
    dot_general x16, matrix products, inner_rows(): lax.dot_general(left, right, (((0,), (0,)), ((), ())), preferred_element_...  110 us
    all_gather x2, waiting for transfers between devices, body(): lax.all_gather(w_qkv[layer_idx], 'grp', axis=0, tiled=True)  104 us
  transfers between devices with their start and end apart: 31, of which 28 were waited for; matrix products, arithmetic and copies ran while one was open for 18% of the time, Pallas kernels for 0%

commit v1 on v0

--- a/solution.py
+++ b/solution.py
@@ -7,6 +7,19 @@
 HDIM = 64
 EPS = 1e-06
 NEGATIVE = -1e30
+
+
+def gather_around(value, axis, dim):
+    ways = lax.axis_size(axis)
+    up = [(d, (d + 1) % ways) for d in range(ways)]
+    down = [(d, (d - 1) % ways) for d in range(ways)]
+    earlier, later = ([value], [value])
+    for _ in range(ways // 2):
+        earlier.append(lax.ppermute(earlier[-1], axis, up))
+    for _ in range((ways - 1) // 2):
+        later.append(lax.ppermute(later[-1], axis, down))
+    line = jnp.concatenate([*earlier[::-1], *later[1:]], axis=dim)
+    return jnp.roll(line, (lax.axis_index(axis) - ways // 2) * value.shape[dim], axis=dim)
 
 
 def norm_apply(values, gains):
@@ -130,7 +143,7 @@
     qkv_low = jnp.dot(normed, w_qkv_full, preferred_element_type=jnp.float32).astype(jnp.bfloat16)
     query = qkv_low[:, :width]
     keys_all, values_all = (
-        lax.all_gather(qkv_low[:, width : 2 * width], "grp", axis=0, tiled=True),
+        gather_around(qkv_low[:, width : 2 * width], "grp", 0),
         lax.all_gather(qkv_low[:, 2 * width :], "grp", axis=0, tiled=True),
     )
     mixed, log_total = attend(

time: 1950 us -> 1970 us (1.010)
  waiting for transfers between devices: 1370 us -> 1270 us
  local copies, waits for them, and re-layouts: 187 us -> 252 us
    ppermute x0 -> x28, waiting for transfers between devices: none -> 162 us  [the longest x16 150 us: gather_around(): earlier.append(lax.ppermute(earlier[-1], axis, up))]
    all_gather x2, waiting for transfers between devices: 139 us -> 61.4 us  [body(): lax.all_gather(w_up[layer_idx], 'grp', axis=0, tiled=True)]
    all_gather x4, waiting for transfers between devices: 73.1 us -> 0.06 us  [layer_forward(): lax.all_gather(qkv_low[:, 2 * width:], 'grp', axis=0, tiled=True)]
    all_gather x4, waiting for transfers between devices: 65.7 us -> 0.06 us  [layer_backward(): lax.all_gather(qkv_low[:, width:2 * width], 'grp', axis=0, tiled=True)]
    unnamed x434 -> x458, local copies, waits for them, and re-layouts: 69.6 us -> 104 us
    reduce_scatter x4, waiting for transfers between devices: 84.8 us -> 60.1 us  [layer_backward(): lax.psum_scatter(key_value_terms.astype(jnp.bfloat16), 'grp', scatter_dim...]
    another operation x8 -> x12, local copies, waits for them, and re-layouts: 50.8 us -> 71.9 us  [split_blocks(): return (whole.reshape(count, width, HEADS, HDIM), width, count)]
    all_gather x2, waiting for transfers between devices: 21 us -> 0.01 us  [body(): lax.all_gather(w_out[layer_idx], 'grp', axis=0, tiled=True)]
  transfers between devices with their start and end apart: 31 -> 59, of which waited for: 28 -> 38; matrix products, arithmetic and copies ran while one was open for 18% -> 25% of each run, Pallas kernels for 0% -> 0%
where the time goes in v1:
time: 1970 us; the launch traced here: 1960 us
  waiting for transfers between devices  1270 us (64%)
  matrix products  305 us (15%)
  local copies, waits for them, and re-layouts  252 us (13%)
  blocking collectives  47 us (2%)
  other arithmetic  44.1 us (2%)
  between operations  20.6 us (1%)
  starting transfers between devices  19.9 us (1%)
    reduce_scatter x2, waiting for transfers between devices, body(): lax.psum_scatter(accum[3].astype(jnp.bfloat16), 'grp', scatter_dimension=...  181 us
    reduce_scatter x2, waiting for transfers between devices, body(): lax.psum_scatter(accum[2].astype(jnp.bfloat16), 'grp', scatter_dimension=...  180 us
    all_gather x2, waiting for transfers between devices, body(): lax.all_gather(w_down[layer_idx], 'grp', axis=0, tiled=True)  153 us
    ppermute x16, waiting for transfers between devices, gather_around(): earlier.append(lax.ppermute(earlier[-1], axis, up))  150 us
    reduce_scatter x2, waiting for transfers between devices, body(): lax.psum_scatter(accum[0].astype(jnp.bfloat16), 'grp', scatter_dimension=...  141 us
    psum x1, waiting for transfers between devices, body(): lax.psum(shards[0].astype(jnp.bfloat16), 'rep').astype(jnp.float32)  132 us
    dot_general x16, matrix products, inner_rows(): lax.dot_general(left, right, (((0,), (0,)), ((), ())), preferred_element_...  110 us
    unnamed x458, local copies, waits for them, and re-layouts  104 us
  transfers between devices with their start and end apart: 59, of which 38 were waited for; matrix products, arithmetic and copies ran while one was open for 25% of the time, Pallas kernels for 0%

profile of v1, /device:TPU:0, one launch (start us, length us, event | category | flops | bytes accessed | tf_op | source)
XLA Modules:
  0.0 1957.1 jit_solution(6013018066608556295)
XLA Ops:
  10.0 13.4 all-gather
  24.2 53.5 %all-gather.43.cloned.1.call-done = bf16[1,1024,3072]{2,1,0:T(8,128)(2,1)} async-done(((bf16[1,128,3072]{2,1,0:T(8,128)(2,1)}), bf16[1,1024,3072]{2,1,0:T(8,128)(2,1)}) %all-gather.43.cloned.1.call-update) | async-done | bytes 6291472 | tf_op jit(solution)/shard_map/all_gather | solution.py:260
  89.3 7.6 collective-permute-done.15
  96.9 7.6 collective-permute-done.16
  104.5 7.6 collective-permute-done.17
  119.9 10.2 collective-permute-done
  130.1 13.2 collective-permute-done.1
  143.3 7.6 collective-permute-done.2
  150.9 7.6 collective-permute-done.3
  167.4 23.6 %all-gather.5 = bf16[1,1024,4]{1,2,0:T(4,128)(2,1)S(1)} all-gather(bf16[1,128,4]{1,2,0:T(4,128)(2,1)S(1)} %get-tuple-element.1637), channel_id=7, replica_groups=mesh['rep'=4,'grp'=8] {'grp'}, dimensions={1}, use_global_device_ids=true | all-gather | bytes 9216 | tf_op jit(solution)/shard_map/all_gather | solution.py:264
  282.9 27.3 %all-gather.47.cloned.1.call-done = bf16[1,1024,4096]{2,1,0:T(8,128)(2,1)} async-done(((bf16[1,128,4096]{2,1,0:T(8,128)(2,1)}), bf16[1,1024,4096]{2,1,0:T(8,128)(2,1)}) %all-gather.47.cloned.1.call-update) | async-done | bytes 8388624 | tf_op jit(solution)/shard_map/all_gather | solution.py:262
  316.3 76.5 %all-gather.49.cloned.1.call-done = bf16[1,4096,1024]{2,1,0:T(8,128)(2,1)} async-done(((bf16[1,512,1024]{2,1,0:T(8,128)(2,1)}), bf16[1,4096,1024]{2,1,0:T(8,128)(2,1)}) %all-gather.49.cloned.1.call-update) | async-done | bytes 8388624 | tf_op jit(solution)/shard_map/all_gather | solution.py:263
  408.6 49.2 %all-gather.51.cloned.1.call-done = bf16[1,1024,3072]{2,1,0:T(8,128)(2,1)} async-done(((bf16[1,128,3072]{2,1,0:T(8,128)(2,1)}), bf16[1,1024,3072]{2,1,0:T(8,128)(2,1)}) %all-gather.51.cloned.1.call-update) | async-done | bytes 6291472 | tf_op jit(solution)/shard_map/all_gather | solution.py:260
  467.5 11.1 collective-permute-done.21
  478.5 13.2 collective-permute-done.22
  499.4 7.7 collective-permute-done.24
  511.6 13.2 collective-permute-done.7
  532.4 7.6 collective-permute-done.9
  540.0 13.2 collective-permute-done.10
  680.1 34.1 %all-gather.55.cloned.1.call-done = bf16[1,1024,4096]{2,1,0:T(8,128)(2,1)} async-done(((bf16[1,128,4096]{2,1,0:T(8,128)(2,1)}), bf16[1,1024,4096]{2,1,0:T(8,128)(2,1)}) %all-gather.55.cloned.1.call-update) | async-done | bytes 8388624 | tf_op jit(solution)/shard_map/all_gather | solution.py:262
  720.3 76.5 %all-gather.57.cloned.1.call-done = bf16[1,4096,1024]{2,1,0:T(8,128)(2,1)} async-done(((bf16[1,512,1024]{2,1,0:T(8,128)(2,1)}), bf16[1,4096,1024]{2,1,0:T(8,128)(2,1)}) %all-gather.57.cloned.1.call-update) | async-done | bytes 8388624 | tf_op jit(solution)/shard_map/all_gather | solution.py:263
  820.4 7.8 fusion.287
  845.7 17.4 while.158
  870.6 18.8 while.156
  918.1 15.1 reduce-scatter.23.cloned.1.call-done
  939.2 44.9 %reduce-scatter.19.cloned.1.call-done = bf16[128,2048]{1,0:T(8,128)(2,1)} async-done(((bf16[1024,2048]{1,0:T(8,128)(2,1)}), bf16[128,2048]{1,0:T(8,128)(2,1)}) %reduce-scatter.19.cloned.1.call-update) | async-done | bytes 524304 | tf_op jit(solution)/shard_map/reduce_scatter | solution.py:233
  1024.8 17.1 while.157
  1051.0 17.6 while.159
  1078.0 9.3 fusion.411
  1087.4 9.7 add_convert_fusion
  1098.2 9.5 fusion.409
  1107.7 11.5 add_convert_fusion.2
  1129.6 9.3 fusion.410
  1138.9 9.6 add_convert_fusion.1
  1149.6 9.5 fusion.408
  1159.1 11.6 add_convert_fusion.3
  1179.3 9.4 add_convert_fusion.5
  1201.9 30.0 %reduce-scatter.31.cloned.1.call-done = bf16[128,1024]{1,0:T(8,128)(2,1)} async-done(((bf16[1024,1024]{1,0:T(8,128)(2,1)}), bf16[128,1024]{1,0:T(8,128)(2,1)}) %reduce-scatter.31.cloned.1.call-update) | async-done | bytes 262160 | tf_op jit(solution)/shard_map/reduce_scatter | solution.py:298
  1231.9 90.5 %reduce-scatter.41.cloned.1.call-done = bf16[512,1024]{1,0:T(8,128)(2,1)} async-done(((bf16[4096,1024]{1,0:T(8,128)(2,1)}), bf16[512,1024]{1,0:T(8,128)(2,1)}) %reduce-scatter.41.cloned.1.call-update) | async-done | bytes 1048592 | tf_op jit(solution)/shard_map/reduce_scatter | solution.py:304
  1322.3 90.1 %reduce-scatter.37.cloned.1.call-done = bf16[128,4096]{1,0:T(8,128)(2,1)} async-done(((bf16[1024,4096]{1,0:T(8,128)(2,1)}), bf16[128,4096]{1,0:T(8,128)(2,1)}) %reduce-scatter.37.cloned.1.call-update) | async-done | bytes 1048592 | tf_op jit(solution)/shard_map/reduce_scatter | solution.py:301
  1412.4 70.5 %reduce-scatter.29.cloned.1.call-done = bf16[128,3072]{1,0:T(8,128)(2,1)} async-done(((bf16[1024,3072]{1,0:T(8,128)(2,1)}), bf16[128,3072]{1,0:T(8,128)(2,1)}) %reduce-scatter.29.cloned.1.call-update) | async-done | bytes 786448 | tf_op jit(solution)/shard_map/reduce_scatter | solution.py:295
  1483.0 90.1 %reduce-scatter.39.cloned.1.call-done = bf16[512,1024]{1,0:T(8,128)(2,1)} async-done(((bf16[4096,1024]{1,0:T(8,128)(2,1)}), bf16[512,1024]{1,0:T(8,128)(2,1)}) %reduce-scatter.39.cloned.1.call-update) | async-done | bytes 1048592 | tf_op jit(solution)/shard_map/reduce_scatter | solution.py:304
  1573.1 90.1 %reduce-scatter.35.cloned.1.call-done = bf16[128,4096]{1,0:T(8,128)(2,1)} async-done(((bf16[1024,4096]{1,0:T(8,128)(2,1)}), bf16[128,4096]{1,0:T(8,128)(2,1)}) %reduce-scatter.35.cloned.1.call-update) | async-done | bytes 1048592 | tf_op jit(solution)/shard_map/reduce_scatter | solution.py:301
  1663.2 70.5 %reduce-scatter.27.cloned.1.call-done = bf16[128,3072]{1,0:T(8,128)(2,1)} async-done(((bf16[1024,3072]{1,0:T(8,128)(2,1)}), bf16[128,3072]{1,0:T(8,128)(2,1)}) %reduce-scatter.27.cloned.1.call-update) | async-done | bytes 786448 | tf_op jit(solution)/shard_map/reduce_scatter | solution.py:295
  1735.6 29.7 %reduce-scatter.45.cloned.1.call-done = bf16[128,4]{1,0:T(8,128)(2,1)} async-done(((bf16[1024,4]{1,0:T(8,128)(2,1)}), bf16[128,4]{1,0:T(8,128)(2,1)}) %reduce-scatter.45.cloned.1.call-update) | async-done | bytes 1040
  1767.5 29.0 %reduce-scatter.43.cloned.1.call-done = bf16[128,4]{1,0:T(8,128)(2,1)} async-done(((bf16[1024,4]{1,0:T(8,128)(2,1)}), bf16[128,4]{1,0:T(8,128)(2,1)}) %reduce-scatter.43.cloned.1.call-update) | async-done | bytes 1040
  1797.4 9.9 all-reduce
  1807.9 132.3 %all-reduce.4.cloned.1.call-done = (bf16[1,128,3072]{2,1,0:T(8,128)(2,1)}, bf16[1,128,3072]{2,1,0:T(8,128)(2,1)}, bf16[1,128,1024]{2,1,0:T(8,128)(2,1)}, bf16[1,...) async-done(((bf16[1,128,3072]{2,1,0:T(8,128)(2,1)}, ...) | async-done | bytes 6291472 | tf_op jit(solution)/shard_map/psum | solution.py:313
  (902 shorter events, 587.6 us)
Async XLA Ops:
  7.2 70.5 %all-gather.43.cloned.1.call-start = ((), (), s32[]{:S(2)}) async-start(), calls=%async_computation.34 | async-start | bytes 7077888 | tf_op jit(solution)/shard_map/all_gather | solution.py:260
  9.9 233.2 %all-gather.31.cloned.1.call-start = ((), (), s32[]{:S(2)}) async-start(), calls=%async_computation.16 | async-start | bytes 2359296 | tf_op jit(solution)/shard_map/all_gather | solution.py:147
  81.6 7.6 collective-permute-start.14
  115.9 139.1 %all-gather.27.cloned.1.call-start = ((), (), s32[]{:S(2)}) async-start(), calls=%async_computation.14 | async-start | bytes 2359296 | tf_op jit(solution)/shard_map/all_gather | solution.py:147
  119.9 10.2 collective-permute-start
  130.1 13.2 collective-permute-start.1
  160.8 110.6 %all-gather.45.cloned.1.call-start = ((), (), s32[]{:S(2)}) async-start(), calls=%async_computation.35 | async-start | bytes 2359296 | tf_op jit(solution)/shard_map/all_gather | solution.py:261
  161.7 148.5 %all-gather.47.cloned.1.call-start = ((), (), s32[]{:S(2)}) async-start(), calls=%async_computation.36 | async-start | bytes 9437184 | tf_op jit(solution)/shard_map/all_gather | solution.py:262
  165.0 227.8 %all-gather.49.cloned.1.call-start = ((), (), s32[]{:S(2)}) async-start(), calls=%async_computation.37 | async-start | bytes 9437184 | tf_op jit(solution)/shard_map/all_gather | solution.py:263
  166.6 291.2 %all-gather.51.cloned.1.call-start = ((), (), s32[]{:S(2)}) async-start(), calls=%async_computation.38 | async-start | bytes 7077888 | tf_op jit(solution)/shard_map/all_gather | solution.py:260
  166.7 24.4 %collective-permute-start.18 = (bf16[128,1024]{1,0:T(8,128)(2,1)S(1)}, bf16[128,1024]{1,0:T(8,128)(2,1)S(1)}, u32[]{:S(2)}, u32[]{:S(2)}) collective-permute-start(bf16[128,1024]{1,0:T(8,128)(2,1)S(1)} %slice.228), channel_id=1, source_target_pairs={{0,7},{1,0},{2,1},{3,2},{4,3},{5,4},{6,5},{7,6},{8,15},{9,8},{10,9... | collective-permute-start | bytes 786440 | tf_op jit(solution)/shard_map/ppermute | solution.py:20
  166.7 24.3 %collective-permute-start.4 = (bf16[128,1024]{1,0:T(8,128)(2,1)S(1)}, bf16[128,1024]{1,0:T(8,128)(2,1)S(1)}, u32[]{:S(2)}, u32[]{:S(2)}) collective-permute-start(bf16[128,1024]{1,0:T(8,128)(2,1)S(1)} %slice.107), channel_id=1, source_target_pairs={{0,7},{1,0},{2,1},{3,2},{4,3},{5,4},{6,5},{7,6},{8,15},{9,8},{10,9... | collective-permute-start | bytes 786440 | tf_op jit(solution)/shard_map/ppermute | solution.py:20
  167.4 451.6 %all-gather.35.cloned.1.call-start = ((), (), s32[]{:S(2)}) async-start(), calls=%async_computation.18 | async-start | bytes 2359296 | tf_op jit(solution)/shard_map/all_gather | solution.py:217
  191.1 11.0 collective-permute-start.5
  194.9 8.7 collective-permute-start.20
  202.1 19.0 collective-permute-start.6
  462.4 168.7 %all-gather.39.cloned.1.call-start = ((), (), s32[]{:S(2)}) async-start(), calls=%async_computation.22 | async-start | bytes 2359296 | tf_op jit(solution)/shard_map/all_gather | solution.py:217
  467.1 175.0 %all-gather.33.cloned.1.call-start = ((), (), s32[]{:S(2)}) async-start(), calls=%async_computation.17 | async-start | bytes 2359296 | tf_op jit(solution)/shard_map/all_gather | solution.py:147
  467.2 11.4 collective-permute-start.21
  478.5 13.2 collective-permute-start.22
  499.4 7.7 collective-permute-start.24
  510.8 147.4 %all-gather.53.cloned.1.call-start = ((), (), s32[]{:S(2)}) async-start(), calls=%async_computation.39 | async-start | bytes 2359296 | tf_op jit(solution)/shard_map/all_gather | solution.py:261
  511.5 149.7 %all-gather.29.cloned.1.call-start = ((), (), s32[]{:S(2)}) async-start(), calls=%async_computation.15 | async-start | bytes 2359296 | tf_op jit(solution)/shard_map/all_gather | solution.py:147
  511.6 13.2 collective-permute-start.7
  540.0 13.2 collective-permute-start.10
  555.4 158.7 %all-gather.55.cloned.1.call-start = ((), (), s32[]{:S(2)}) async-start(), calls=%async_computation.40 | async-start | bytes 9437184 | tf_op jit(solution)/shard_map/all_gather | solution.py:262
  556.2 240.6 %all-gather.57.cloned.1.call-start = ((), (), s32[]{:S(2)}) async-start(), calls=%async_computation.41 | async-start | bytes 9437184 | tf_op jit(solution)/shard_map/all_gather | solution.py:263
  556.8 332.8 %all-gather.37.cloned.1.call-start = ((), (), s32[]{:S(2)}) async-start(), calls=%async_computation.20 | async-start | bytes 2359296 | tf_op jit(solution)/shard_map/all_gather | solution.py:217
  557.3 343.1 %all-gather.41.cloned.1.call-start = ((), (), s32[]{:S(2)}) async-start(), calls=%async_computation.24 | async-start | bytes 2359296 | tf_op jit(solution)/shard_map/all_gather | solution.py:217
  557.5 8.3 collective-permute-start.11
  565.8 7.7 collective-permute-start.12
  569.6 12.2 collective-permute-start.27
  573.4 359.8 %reduce-scatter.23.cloned.1.call-start = ((), (), s32[]{:S(2)}) async-start(), calls=%async_computation.23 | async-start | bytes 4718592 | tf_op jit(solution)/shard_map/reduce_scatter | solution.py:233
  573.4 25.8 %collective-permute-start.13 = (bf16[128,1024]{1,0:T(8,128)(2,1)}, bf16[128,1024]{1,0:T(8,128)(2,1)}, u32[]{:S(2)}, u32[]{:S(2)}) collective-permute-start(bf16[128,1024]{1,0:T(8,128)(2,1)} %collective-permute-done.12), channel_id=1, source_target_pairs={{0,7},{1,0},{2,1},{3,2},{4,3},{5,4},{6,5},{7,6},{8,15},{9,8},{10,9... | collective-permute-start | bytes 786440 | tf_op jit(solution)/shard_map/ppermute | solution.py:20
  867.2 116.9 %reduce-scatter.19.cloned.1.call-start = ((), (), s32[]{:S(2)}) async-start(), calls=%async_computation.19 | async-start | bytes 4718592 | tf_op jit(solution)/shard_map/reduce_scatter | solution.py:233
  889.4 282.0 %reduce-scatter.21.cloned.1.call-start = ((), (), s32[]{:S(2)}) async-start(), calls=%async_computation.21 | async-start | bytes 4718592 | tf_op jit(solution)/shard_map/reduce_scatter | solution.py:233
  1042.0 137.3 %reduce-scatter.25.cloned.1.call-start = ((), (), s32[]{:S(2)}) async-start(), calls=%async_computation.25 | async-start | bytes 4718592 | tf_op jit(solution)/shard_map/reduce_scatter | solution.py:233
  1068.7 133.1 %reduce-scatter.33.cloned.1.call-start = ((), (), s32[]{:S(2)}) async-start(), calls=%async_computation.29 | async-start | bytes 2359296 | tf_op jit(solution)/shard_map/reduce_scatter | solution.py:298
  1072.6 159.3 %reduce-scatter.31.cloned.1.call-start = ((), (), s32[]{:S(2)}) async-start(), calls=%async_computation.28 | async-start | bytes 2359296 | tf_op jit(solution)/shard_map/reduce_scatter | solution.py:298
  1076.5 245.9 %reduce-scatter.41.cloned.1.call-start = ((), (), s32[]{:S(2)}) async-start(), calls=%async_computation.33 | async-start | bytes 9437184 | tf_op jit(solution)/shard_map/reduce_scatter | solution.py:304
  1097.2 315.3 %reduce-scatter.37.cloned.1.call-start = ((), (), s32[]{:S(2)}) async-start(), calls=%async_computation.31 | async-start | bytes 9437184 | tf_op jit(solution)/shard_map/reduce_scatter | solution.py:301
  1119.3 363.7 %reduce-scatter.29.cloned.1.call-start = ((), (), s32[]{:S(2)}) async-start(), calls=%async_computation.27 | async-start | bytes 7077888 | tf_op jit(solution)/shard_map/reduce_scatter | solution.py:295
  1128.0 445.1 %reduce-scatter.39.cloned.1.call-start = ((), (), s32[]{:S(2)}) async-start(), calls=%async_computation.32 | async-start | bytes 9437184 | tf_op jit(solution)/shard_map/reduce_scatter | solution.py:304
  1148.6 514.6 %reduce-scatter.35.cloned.1.call-start = ((), (), s32[]{:S(2)}) async-start(), calls=%async_computation.30 | async-start | bytes 9437184 | tf_op jit(solution)/shard_map/reduce_scatter | solution.py:301
  1170.7 563.0 %reduce-scatter.27.cloned.1.call-start = ((), (), s32[]{:S(2)}) async-start(), calls=%async_computation.26 | async-start | bytes 7077888 | tf_op jit(solution)/shard_map/reduce_scatter | solution.py:295
  1188.8 576.4 %reduce-scatter.45.cloned.1.call-start = ((), (), s32[]{:S(2)}) async-start(), calls=%async_computation.43 | async-start | bytes 294912
  1190.4 606.1 %reduce-scatter.43.cloned.1.call-start = ((), (), s32[]{:S(2)}) async-start(), calls=%async_computation.42 | async-start | bytes 294912
  1201.8 738.4 %all-reduce.4.cloned.1.call-start = ((), (), s32[]{:S(2)}) async-start(), calls=%async_computation.44 | async-start | bytes 12582912 | tf_op jit(solution)/shard_map/psum | solution.py:313
  (241 other events, 4515.4 us)
Sparse Core Ops, SparseCore 0:
  10.2 67.4 all-gather.42
  116.0 32.7 all-gather.30
  160.9 29.6 all-gather.26
  192.6 32.6 all-gather.44
  226.8 83.3 all-gather.46
  312.2 80.5 all-gather.48
  394.5 63.2 all-gather.50
  462.6 33.6 all-gather.34
  497.9 30.2 all-gather.38
  529.7 34.4 all-gather.32
  565.8 31.9 all-gather.52
  599.2 31.7 all-gather.28
  632.6 81.5 all-gather.54
  716.2 80.5 all-gather.56
  798.3 27.6 all-gather.36
  827.4 28.6 all-gather.40
  867.3 65.8 reduce-scatter.22
  935.9 48.1 reduce-scatter.18
  1042.2 64.9 reduce-scatter.20
  1109.9 48.1 reduce-scatter.24
  1160.9 33.9 reduce-scatter.32
  1197.2 34.6 reduce-scatter.30
  1234.2 88.1 reduce-scatter.40
  1324.5 87.9 reduce-scatter.36
  1414.7 68.1 reduce-scatter.28
  1485.1 87.9 reduce-scatter.38
  1575.2 87.9 reduce-scatter.34
  1665.5 68.1 reduce-scatter.26
  1736.5 28.6 reduce-scatter.44
  1768.0 28.4 reduce-scatter.42
  1801.0 139.1 all-reduce.3
